TPU v7x, 128 devices: a whole 4x4x4 slice. The times are simulated.
128 devices in a mesh: ctx: 32 (over y, x, z_lo), batch: 4 (over z_hi, core).
Axes of the slice: x: 4, y: 4, z: 4 (z_hi: 2, z_lo: 2; z = z_hi * 2 + z_lo), core: 2. Of those that a mesh axis runs over, the one named last changes fastest.
Arguments:
- queries: bfloat16 [4, 8192, 2048], P('batch', 'ctx'), may hold values from -120 to 120
- keys: bfloat16 [4, 8192, 512], P('batch', 'ctx'), may hold values from -6 to 6
- values: bfloat16 [4, 8192, 512], P('batch', 'ctx'), may hold values from -6 to 6
- tau: float32 [16], replicated, may hold values from 0.5 to 2
- out_grad: bfloat16 [4, 8192, 2048], P('batch', 'ctx'), may hold values from -18 to 18
- key_blocks: int32 [4, 64, 13], replicated, may hold values from 0 to 63, as said below
Outputs:
- attended: bfloat16 [4, 8192, 2048], P('batch', 'ctx')
- query_grad: bfloat16 [4, 8192, 2048], P('batch', 'ctx')
- key_grad: bfloat16 [4, 8192, 512], P('batch', 'ctx')
- value_grad: bfloat16 [4, 8192, 512], P('batch', 'ctx')
- tau_grad: float32 [16], replicated
Inputs may be any that keep to these rules, and one draw needn't show every extreme that they name: `key_blocks`: row a of head group g lists a - 1, a, a + 1, then a + m s and a - m s for m = 1 to 5, all modulo 64, with a stride s of 2 or 3 drawn for each group and row.
All inputs are finite; a program needn't handle non-finite values.
Results may differ from a plain program's by a relative error of at most 0.0051.
Values may be sent and summed in bfloat16 or wider, within the bound.
A program may use at most 192 MiB of HBM per device.

v0:
```python
import math
import jax
import jax.numpy as jnp
from jax import lax
from jax.sharding import PartitionSpec as P

HEADS = 16
KV_HEADS = 4
HD = 128
BLOCK = 128


def passed_along(block, axis, distance):
    devices = range(lax.axis_size(axis))
    route = [((i - distance) % len(devices), i) for i in devices]
    return lax.ppermute(block, axis, route)


def body(queries, keys, values, tau, out_grad, key_blocks):
    ctx_size = lax.axis_size("ctx")
    myself = lax.axis_index("ctx")
    tokens = queries.shape[1]
    local_blocks = tokens // BLOCK
    listed_count = key_blocks.shape[2]
    block_reach = 3 * ((listed_count - 3) // 2)
    reach_dev = min((local_blocks - 1 + block_reach) // local_blocks, ctx_size // 2)
    slot_count = 2 * reach_dev + 1
    per_group = HEADS // KV_HEADS
    root_hd = math.sqrt(HD)
    paired = jnp.stack([keys[0], values[0]])
    window = jnp.zeros((2, slot_count, tokens, KV_HEADS * HD), jnp.bfloat16)
    farthest = passed_along(paired, "ctx", -reach_dev)
    window = lax.dynamic_update_slice_in_dim(window, farthest[:, None], slot_count - 1, 1)

    def walk_turn(turn_no, state_in):
        current, filled = state_in
        current = passed_along(current, "ctx", 1)
        filled = lax.dynamic_update_slice_in_dim(
            filled, current[:, None], slot_count - 1 - turn_no, 1
        )
        return (current, filled)

    window = lax.fori_loop(1, slot_count, walk_turn, (farthest, window))[1]
    blocks_all = window.reshape(2, slot_count * local_blocks, BLOCK, KV_HEADS, HD)
    own_lists = lax.dynamic_slice_in_dim(key_blocks, myself * local_blocks, local_blocks, 1)
    window_index = (
        own_lists // local_blocks - myself + reach_dev
    ) % ctx_size * local_blocks + own_lists % local_blocks
    window_ids = jnp.arange(slot_count * local_blocks, dtype=jnp.int32)
    query_all = queries[0].reshape(local_blocks, BLOCK, KV_HEADS, per_group, HD)
    grad_all = out_grad[0].reshape(local_blocks, BLOCK, KV_HEADS, per_group, HD)
    factor = tau.reshape(KV_HEADS, per_group) / root_hd
    results = []
    query_parts = []
    placed_parts = []
    scale_parts = []
    for group_id in range(KV_HEADS):
        picks = window_index[group_id].reshape(-1)
        key_rows = jnp.take(blocks_all[0, :, :, group_id], picks, axis=0).reshape(
            local_blocks, listed_count * BLOCK, HD
        )
        value_rows = jnp.take(blocks_all[1, :, :, group_id], picks, axis=0).reshape(
            local_blocks, listed_count * BLOCK, HD
        )
        query_rows = query_all[:, :, group_id]
        grad_rows = grad_all[:, :, group_id]
        scale_row = factor[group_id]
        raw_scores = jnp.einsum(
            "nqhd,nkd->nhqk", query_rows, key_rows, preferred_element_type=jnp.float32
        )
        weights = jax.nn.softmax(raw_scores * scale_row[None, :, None, None], axis=-1)
        probs_low = weights.astype(jnp.bfloat16)
        result = jnp.einsum(
            "nhqk,nkd->nqhd", probs_low, value_rows, preferred_element_type=jnp.float32
        )
        row_dot = jnp.sum(grad_rows.astype(jnp.float32) * result, axis=-1)
        dweights = jnp.einsum(
            "nqhd,nkd->nhqk", grad_rows, value_rows, preferred_element_type=jnp.float32
        )
        dscores = weights * (dweights - row_dot.transpose(0, 2, 1)[..., None])
        scale_parts.append(jnp.sum(dscores * raw_scores, axis=(0, 2, 3)) / root_hd)
        scaled = (dscores * scale_row[None, :, None, None]).astype(jnp.bfloat16)
        query_part = jnp.einsum(
            "nhqk,nkd->nqhd", scaled, key_rows, preferred_element_type=jnp.float32
        )
        key_part = jnp.einsum(
            "nhqk,nqhd->nkd", scaled, query_rows, preferred_element_type=jnp.float32
        )
        value_part = jnp.einsum(
            "nhqk,nqhd->nkd", probs_low, grad_rows, preferred_element_type=jnp.float32
        )
        chooser = (picks[:, None] == window_ids[None, :]).astype(jnp.float32)
        both_parts = jnp.stack([key_part, value_part]).reshape(
            2, local_blocks * listed_count, BLOCK * HD
        )
        placed_parts.append(
            jnp.einsum("sw,csx->cwx", chooser, both_parts, precision=lax.Precision.HIGHEST)
        )
        results.append(result)
        query_parts.append(query_part)
    attended = jnp.stack(results, axis=2).reshape(1, tokens, HEADS * HD).astype(jnp.bfloat16)
    query_grad = jnp.stack(query_parts, axis=2).reshape(1, tokens, HEADS * HD).astype(jnp.bfloat16)
    stacked = jnp.stack(placed_parts).reshape(KV_HEADS, 2, slot_count, local_blocks, BLOCK, HD)
    grads_window = stacked.transpose(2, 1, 3, 4, 0, 5).reshape(slot_count, 2, tokens, KV_HEADS * HD)

    def chain_turn(turn_no, partial_sum):
        moved = passed_along(partial_sum, "ctx", -1)
        return moved + lax.dynamic_index_in_dim(grads_window, turn_no, 0, keepdims=False)

    partial_sum = lax.fori_loop(1, slot_count, chain_turn, grads_window[0])
    summed = passed_along(partial_sum.astype(jnp.bfloat16), "ctx", reach_dev).astype(
        partial_sum.dtype
    )
    key_grad = summed[0].reshape(1, tokens, KV_HEADS * HD).astype(jnp.bfloat16)
    value_grad = summed[1].reshape(1, tokens, KV_HEADS * HD).astype(jnp.bfloat16)
    scale_total = lax.psum(jnp.stack(scale_parts), ("ctx", "batch"))
    tau_grad = scale_total.reshape(HEADS) / math.sqrt(lax.axis_size("batch") * ctx_size * tokens)
    return (attended, query_grad, key_grad, value_grad, tau_grad)


def solution(mesh):
    return jax.shard_map(
        body,
        mesh=mesh,
        in_specs=(
            P("batch", "ctx", None),
            P("batch", "ctx", None),
            P("batch", "ctx", None),
            P(),
            P("batch", "ctx", None),
            P(),
        ),
        out_specs=(
            P("batch", "ctx", None),
            P("batch", "ctx", None),
            P("batch", "ctx", None),
            P("batch", "ctx", None),
            P(),
        ),
        check_vma=False,
    )
```

profile of v0, /device:TPU:0, one launch (start us, length us, event | category | flops | bytes accessed | tf_op | source)
XLA Modules:
  0.0 1086.7 jit_solution(6687766181752277367)
XLA Ops:
  17.2 5.5 dynamic_update_slice.10
  22.7 280.8 %while.30 = (s32[]{:T(128)}, bf16[2,256,512]{2,1,0:T(8,128)(2,1)}, bf16[2,17,256,512]{3,2,0,1:T(8,128)(2,1)}, s32[]{:T(128)}, s32[]{:T(128)}, /*index=5*/s32[]{:T(128)}, s32[]{:T(128)}) while((s32[]{:T(128)}, bf16[2,256,512]{2,1,0:T(8,128)(2,1)}, bf16[2,17,256,512]{3,2,0,1:T(8,128)(2,1)}, s32[]{:T(128)}, s32[]{:T(128)}, /*index=5*/s32[]{:T(128)}, ...), condition=%wide.region_1.0_spmd, body=%wide.region_0.0_spmd.sunk | while | flops 6 | bytes 4194471 | solution.py:43
  24.7 16.6 %collective-permute-done = bf16[2,256,512]{2,1,0:T(8,128)(2,1)S(1)} collective-permute-done((bf16[2,256,512]{2,1,0:T(8,128)(2,1)}, bf16[2,256,512]{2,1,0:T(8,128)(2,1)S(1)}, u32[]{:S(2)}, u32[]{:S(2)}) %collective-permute-start) | collective-permute-done | bytes 524320 | tf_op jit(solution)/shard_map/while/body/eval_jaxpr/ppermute | solution.py:16
  42.9 16.6 %collective-permute-done = bf16[2,256,512]{2,1,0:T(8,128)(2,1)S(1)} collective-permute-done((bf16[2,256,512]{2,1,0:T(8,128)(2,1)}, bf16[2,256,512]{2,1,0:T(8,128)(2,1)S(1)}, u32[]{:S(2)}, u32[]{:S(2)}) %collective-permute-start) | collective-permute-done | bytes 524320 | tf_op jit(solution)/shard_map/while/body/eval_jaxpr/ppermute | solution.py:16
  61.2 15.7 %collective-permute-done = bf16[2,256,512]{2,1,0:T(8,128)(2,1)S(1)} collective-permute-done((bf16[2,256,512]{2,1,0:T(8,128)(2,1)}, bf16[2,256,512]{2,1,0:T(8,128)(2,1)S(1)}, u32[]{:S(2)}, u32[]{:S(2)}) %collective-permute-start) | collective-permute-done | bytes 524320 | tf_op jit(solution)/shard_map/while/body/eval_jaxpr/ppermute | solution.py:16
  78.5 14.7 %collective-permute-done = bf16[2,256,512]{2,1,0:T(8,128)(2,1)S(1)} collective-permute-done((bf16[2,256,512]{2,1,0:T(8,128)(2,1)}, bf16[2,256,512]{2,1,0:T(8,128)(2,1)S(1)}, u32[]{:S(2)}, u32[]{:S(2)}) %collective-permute-start) | collective-permute-done | bytes 524320 | tf_op jit(solution)/shard_map/while/body/eval_jaxpr/ppermute | solution.py:16
  94.8 13.8 %collective-permute-done = bf16[2,256,512]{2,1,0:T(8,128)(2,1)S(1)} collective-permute-done((bf16[2,256,512]{2,1,0:T(8,128)(2,1)}, bf16[2,256,512]{2,1,0:T(8,128)(2,1)S(1)}, u32[]{:S(2)}, u32[]{:S(2)}) %collective-permute-start) | collective-permute-done | bytes 524320 | tf_op jit(solution)/shard_map/while/body/eval_jaxpr/ppermute | solution.py:16
  110.3 13.6 %collective-permute-done = bf16[2,256,512]{2,1,0:T(8,128)(2,1)S(1)} collective-permute-done((bf16[2,256,512]{2,1,0:T(8,128)(2,1)}, bf16[2,256,512]{2,1,0:T(8,128)(2,1)S(1)}, u32[]{:S(2)}, u32[]{:S(2)}) %collective-permute-start) | collective-permute-done | bytes 524320 | tf_op jit(solution)/shard_map/while/body/eval_jaxpr/ppermute | solution.py:16
  125.5 13.6 %collective-permute-done = bf16[2,256,512]{2,1,0:T(8,128)(2,1)S(1)} collective-permute-done((bf16[2,256,512]{2,1,0:T(8,128)(2,1)}, bf16[2,256,512]{2,1,0:T(8,128)(2,1)S(1)}, u32[]{:S(2)}, u32[]{:S(2)}) %collective-permute-start) | collective-permute-done | bytes 524320 | tf_op jit(solution)/shard_map/while/body/eval_jaxpr/ppermute | solution.py:16
  140.8 13.7 %collective-permute-done = bf16[2,256,512]{2,1,0:T(8,128)(2,1)S(1)} collective-permute-done((bf16[2,256,512]{2,1,0:T(8,128)(2,1)}, bf16[2,256,512]{2,1,0:T(8,128)(2,1)S(1)}, u32[]{:S(2)}, u32[]{:S(2)}) %collective-permute-start) | collective-permute-done | bytes 524320 | tf_op jit(solution)/shard_map/while/body/eval_jaxpr/ppermute | solution.py:16
  156.1 14.8 %collective-permute-done = bf16[2,256,512]{2,1,0:T(8,128)(2,1)S(1)} collective-permute-done((bf16[2,256,512]{2,1,0:T(8,128)(2,1)}, bf16[2,256,512]{2,1,0:T(8,128)(2,1)S(1)}, u32[]{:S(2)}, u32[]{:S(2)}) %collective-permute-start) | collective-permute-done | bytes 524320 | tf_op jit(solution)/shard_map/while/body/eval_jaxpr/ppermute | solution.py:16
  172.5 15.9 %collective-permute-done = bf16[2,256,512]{2,1,0:T(8,128)(2,1)S(1)} collective-permute-done((bf16[2,256,512]{2,1,0:T(8,128)(2,1)}, bf16[2,256,512]{2,1,0:T(8,128)(2,1)S(1)}, u32[]{:S(2)}, u32[]{:S(2)}) %collective-permute-start) | collective-permute-done | bytes 524320 | tf_op jit(solution)/shard_map/while/body/eval_jaxpr/ppermute | solution.py:16
  190.0 17.0 %collective-permute-done = bf16[2,256,512]{2,1,0:T(8,128)(2,1)S(1)} collective-permute-done((bf16[2,256,512]{2,1,0:T(8,128)(2,1)}, bf16[2,256,512]{2,1,0:T(8,128)(2,1)S(1)}, u32[]{:S(2)}, u32[]{:S(2)}) %collective-permute-start) | collective-permute-done | bytes 524320 | tf_op jit(solution)/shard_map/while/body/eval_jaxpr/ppermute | solution.py:16
  208.6 18.1 %collective-permute-done = bf16[2,256,512]{2,1,0:T(8,128)(2,1)S(1)} collective-permute-done((bf16[2,256,512]{2,1,0:T(8,128)(2,1)}, bf16[2,256,512]{2,1,0:T(8,128)(2,1)S(1)}, u32[]{:S(2)}, u32[]{:S(2)}) %collective-permute-start) | collective-permute-done | bytes 524320 | tf_op jit(solution)/shard_map/while/body/eval_jaxpr/ppermute | solution.py:16
  228.3 19.2 %collective-permute-done = bf16[2,256,512]{2,1,0:T(8,128)(2,1)S(1)} collective-permute-done((bf16[2,256,512]{2,1,0:T(8,128)(2,1)}, bf16[2,256,512]{2,1,0:T(8,128)(2,1)S(1)}, u32[]{:S(2)}, u32[]{:S(2)}) %collective-permute-start) | collective-permute-done | bytes 524320 | tf_op jit(solution)/shard_map/while/body/eval_jaxpr/ppermute | solution.py:16
  249.1 18.4 %collective-permute-done = bf16[2,256,512]{2,1,0:T(8,128)(2,1)S(1)} collective-permute-done((bf16[2,256,512]{2,1,0:T(8,128)(2,1)}, bf16[2,256,512]{2,1,0:T(8,128)(2,1)S(1)}, u32[]{:S(2)}, u32[]{:S(2)}) %collective-permute-start) | collective-permute-done | bytes 524320 | tf_op jit(solution)/shard_map/while/body/eval_jaxpr/ppermute | solution.py:16
  269.1 17.5 %collective-permute-done = bf16[2,256,512]{2,1,0:T(8,128)(2,1)S(1)} collective-permute-done((bf16[2,256,512]{2,1,0:T(8,128)(2,1)}, bf16[2,256,512]{2,1,0:T(8,128)(2,1)S(1)}, u32[]{:S(2)}, u32[]{:S(2)}) %collective-permute-start) | collective-permute-done | bytes 524320 | tf_op jit(solution)/shard_map/while/body/eval_jaxpr/ppermute | solution.py:16
  288.3 13.6 %collective-permute-done = bf16[2,256,512]{2,1,0:T(8,128)(2,1)S(1)} collective-permute-done((bf16[2,256,512]{2,1,0:T(8,128)(2,1)}, bf16[2,256,512]{2,1,0:T(8,128)(2,1)S(1)}, u32[]{:S(2)}, u32[]{:S(2)}) %collective-permute-start) | collective-permute-done | bytes 524320 | tf_op jit(solution)/shard_map/while/body/eval_jaxpr/ppermute | solution.py:16
  303.5 8.0 copy.85
  311.5 13.3 %reshape.174 = bf16[2,34,128,4,128]{4,3,2,1,0:T(4,128)(2,1)} reshape(bf16[2,17,256,512]{3,2,1,0:T(8,128)(2,1)} %copy.85) | data formatting | bytes 17825792 | tf_op jit(solution)/shard_map/reshape | solution.py:44
  324.9 23.1 %fusion.82 = (bf16[1,34,128,1,128]{4,3,2,1,0:T(2,128)(2,1)S(1)}, bf16[1,34,128,1,128]{4,3,2,1,0:T(2,128)(2,1)}, bf16[1,34,128,1,128]{4,3,2,1,0:T(2,128)(2,1)}, b...) fusion(bf16[2,34,128,4,128]{4,3,2,1,0:T(4,128)(2,1)} %reshape.174), kind=kLoop, calls=%fused_computation.196 | loop fusion | bytes 17825792 | tf_op jit(solution)/shard_map/slice | solution.py:59
  390.2 4.9 fusion.58
  424.4 4.9 fusion.59
  459.8 6.5 convolution_bitcast_fusion.2
  474.9 6.5 convolution_bitcast_fusion.1
  513.1 4.9 convolution_bitcast_fusion
  522.3 63.8 %psum.7 = f32[4,4]{1,0:T(4,128)S(1)} all-reduce(f32[4,4]{1,0:T(4,128)S(1)} %pad_maximum_fusion.3), channel_id=1, replica_groups=mesh['ctx'=32,'batch'=4] {'ctx','batch'}, use_global_device_ids=true, to_apply=%region_20.22 | all-reduce | flops 16 | bytes 128 | tf_op jit(solution)/shard_map/psum | solution.py:116
  588.4 5.2 convolution_bitcast_fusion.11
  596.3 6.5 convolution_bitcast_fusion.3
  614.7 6.9 copy.256
  621.6 20.0 %copy.128 = f32[17,2,2,128,4,128]{5,4,3,2,1,0:T(4,128)} copy(f32[17,2,2,128,4,128]{5,3,2,0,1,4:T(8,128)S(1)} %bitcast.371) | data formatting | bytes 35651584 | tf_op jit(solution)/shard_map/transpose | solution.py:104
  641.6 21.9 %reshape.183 = f32[17,2,256,512]{3,2,1,0:T(8,128)} reshape(f32[17,2,2,128,4,128]{5,4,3,2,1,0:T(4,128)} %copy.128) | data formatting | bytes 35651584 | tf_op jit(solution)/shard_map/reshape | solution.py:104
  665.9 406.7 %while.31 = (s32[]{:T(128)}, f32[2,256,512]{2,1,0:T(8,128)S(1)}, f32[17,2,256,512]{3,2,1,0:T(8,128)}, s32[]{:T(128)}, s32[]{:T(128)}, /*index=5*/s32[]{:T(128)}) while((s32[]{:T(128)}, f32[2,256,512]{2,1,0:T(8,128)S(1)}, f32[17,2,256,512]{3,2,1,0:T(8,128)}, s32[]{:T(128)}, s32[]{:T(128)}, /*index=5*/s32[]{:T(128)}) %tuple.109), condition=%wide.region_15.17_spmd, body=%wide.region_14.16_spmd.sunk | while | flops 262149 | bytes 7340179 | solution.py:110
  666.8 23.6 %collective-permute-done.1 = f32[2,256,512]{2,1,0:T(8,128)S(1)} collective-permute-done((f32[2,256,512]{2,1,0:T(8,128)S(1)}, f32[2,256,512]{2,1,0:T(8,128)S(1)}, u32[]{:S(2)}, u32[]{:S(2)}) %collective-permute-start.1) | collective-permute-done | bytes 1048608 | tf_op jit(solution)/shard_map/while/body/eval_jaxpr/ppermute | solution.py:16
  691.9 6.0 collective-permute-start.1
  697.9 22.1 %collective-permute-done.1 = f32[2,256,512]{2,1,0:T(8,128)S(1)} collective-permute-done((f32[2,256,512]{2,1,0:T(8,128)S(1)}, f32[2,256,512]{2,1,0:T(8,128)S(1)}, u32[]{:S(2)}, u32[]{:S(2)}) %collective-permute-start.1) | collective-permute-done | bytes 1048608 | tf_op jit(solution)/shard_map/while/body/eval_jaxpr/ppermute | solution.py:16
  721.4 6.8 collective-permute-start.1
  728.2 21.2 %collective-permute-done.1 = f32[2,256,512]{2,1,0:T(8,128)S(1)} collective-permute-done((f32[2,256,512]{2,1,0:T(8,128)S(1)}, f32[2,256,512]{2,1,0:T(8,128)S(1)}, u32[]{:S(2)}, u32[]{:S(2)}) %collective-permute-start.1) | collective-permute-done | bytes 1048608 | tf_op jit(solution)/shard_map/while/body/eval_jaxpr/ppermute | solution.py:16
  750.8 6.8 collective-permute-start.1
  757.5 20.2 %collective-permute-done.1 = f32[2,256,512]{2,1,0:T(8,128)S(1)} collective-permute-done((f32[2,256,512]{2,1,0:T(8,128)S(1)}, f32[2,256,512]{2,1,0:T(8,128)S(1)}, u32[]{:S(2)}, u32[]{:S(2)}) %collective-permute-start.1) | collective-permute-done | bytes 1048608 | tf_op jit(solution)/shard_map/while/body/eval_jaxpr/ppermute | solution.py:16
  779.2 6.8 collective-permute-start.1
  786.0 19.3 %collective-permute-done.1 = f32[2,256,512]{2,1,0:T(8,128)S(1)} collective-permute-done((f32[2,256,512]{2,1,0:T(8,128)S(1)}, f32[2,256,512]{2,1,0:T(8,128)S(1)}, u32[]{:S(2)}, u32[]{:S(2)}) %collective-permute-start.1) | collective-permute-done | bytes 1048608 | tf_op jit(solution)/shard_map/while/body/eval_jaxpr/ppermute | solution.py:16
  806.7 6.8 collective-permute-start.1
  813.5 18.4 %collective-permute-done.1 = f32[2,256,512]{2,1,0:T(8,128)S(1)} collective-permute-done((f32[2,256,512]{2,1,0:T(8,128)S(1)}, f32[2,256,512]{2,1,0:T(8,128)S(1)}, u32[]{:S(2)}, u32[]{:S(2)}) %collective-permute-start.1) | collective-permute-done | bytes 1048608 | tf_op jit(solution)/shard_map/while/body/eval_jaxpr/ppermute | solution.py:16
  833.3 6.8 collective-permute-start.1
  840.1 17.5 %collective-permute-done.1 = f32[2,256,512]{2,1,0:T(8,128)S(1)} collective-permute-done((f32[2,256,512]{2,1,0:T(8,128)S(1)}, f32[2,256,512]{2,1,0:T(8,128)S(1)}, u32[]{:S(2)}, u32[]{:S(2)}) %collective-permute-start.1) | collective-permute-done | bytes 1048608 | tf_op jit(solution)/shard_map/while/body/eval_jaxpr/ppermute | solution.py:16
  859.0 6.8 collective-permute-start.1
  865.8 16.5 %collective-permute-done.1 = f32[2,256,512]{2,1,0:T(8,128)S(1)} collective-permute-done((f32[2,256,512]{2,1,0:T(8,128)S(1)}, f32[2,256,512]{2,1,0:T(8,128)S(1)}, u32[]{:S(2)}, u32[]{:S(2)}) %collective-permute-start.1) | collective-permute-done | bytes 1048608 | tf_op jit(solution)/shard_map/while/body/eval_jaxpr/ppermute | solution.py:16
  883.8 6.8 collective-permute-start.1
  890.5 15.6 %collective-permute-done.1 = f32[2,256,512]{2,1,0:T(8,128)S(1)} collective-permute-done((f32[2,256,512]{2,1,0:T(8,128)S(1)}, f32[2,256,512]{2,1,0:T(8,128)S(1)}, u32[]{:S(2)}, u32[]{:S(2)}) %collective-permute-start.1) | collective-permute-done | bytes 1048608 | tf_op jit(solution)/shard_map/while/body/eval_jaxpr/ppermute | solution.py:16
  907.6 6.8 collective-permute-start.1
  914.4 15.1 %collective-permute-done.1 = f32[2,256,512]{2,1,0:T(8,128)S(1)} collective-permute-done((f32[2,256,512]{2,1,0:T(8,128)S(1)}, f32[2,256,512]{2,1,0:T(8,128)S(1)}, u32[]{:S(2)}, u32[]{:S(2)}) %collective-permute-start.1) | collective-permute-done | bytes 1048608 | tf_op jit(solution)/shard_map/while/body/eval_jaxpr/ppermute | solution.py:16
  930.9 6.8 collective-permute-start.1
  937.7 15.1 %collective-permute-done.1 = f32[2,256,512]{2,1,0:T(8,128)S(1)} collective-permute-done((f32[2,256,512]{2,1,0:T(8,128)S(1)}, f32[2,256,512]{2,1,0:T(8,128)S(1)}, u32[]{:S(2)}, u32[]{:S(2)}) %collective-permute-start.1) | collective-permute-done | bytes 1048608 | tf_op jit(solution)/shard_map/while/body/eval_jaxpr/ppermute | solution.py:16
  954.3 6.8 collective-permute-start.1
  961.0 15.1 %collective-permute-done.1 = f32[2,256,512]{2,1,0:T(8,128)S(1)} collective-permute-done((f32[2,256,512]{2,1,0:T(8,128)S(1)}, f32[2,256,512]{2,1,0:T(8,128)S(1)}, u32[]{:S(2)}, u32[]{:S(2)}) %collective-permute-start.1) | collective-permute-done | bytes 1048608 | tf_op jit(solution)/shard_map/while/body/eval_jaxpr/ppermute | solution.py:16
  977.6 6.8 collective-permute-start.1
  984.4 15.5 %collective-permute-done.1 = f32[2,256,512]{2,1,0:T(8,128)S(1)} collective-permute-done((f32[2,256,512]{2,1,0:T(8,128)S(1)}, f32[2,256,512]{2,1,0:T(8,128)S(1)}, u32[]{:S(2)}, u32[]{:S(2)}) %collective-permute-start.1) | collective-permute-done | bytes 1048608 | tf_op jit(solution)/shard_map/while/body/eval_jaxpr/ppermute | solution.py:16
  1001.3 6.8 collective-permute-start.1
  1008.1 16.6 %collective-permute-done.1 = f32[2,256,512]{2,1,0:T(8,128)S(1)} collective-permute-done((f32[2,256,512]{2,1,0:T(8,128)S(1)}, f32[2,256,512]{2,1,0:T(8,128)S(1)}, u32[]{:S(2)}, u32[]{:S(2)}) %collective-permute-start.1) | collective-permute-done | bytes 1048608 | tf_op jit(solution)/shard_map/while/body/eval_jaxpr/ppermute | solution.py:16
  1026.1 6.8 collective-permute-start.1
  1032.9 17.7 %collective-permute-done.1 = f32[2,256,512]{2,1,0:T(8,128)S(1)} collective-permute-done((f32[2,256,512]{2,1,0:T(8,128)S(1)}, f32[2,256,512]{2,1,0:T(8,128)S(1)}, u32[]{:S(2)}, u32[]{:S(2)}) %collective-permute-start.1) | collective-permute-done | bytes 1048608 | tf_op jit(solution)/shard_map/while/body/eval_jaxpr/ppermute | solution.py:16
  1052.0 6.8 collective-permute-start.1
  1058.8 12.3 %collective-permute-done.1 = f32[2,256,512]{2,1,0:T(8,128)S(1)} collective-permute-done((f32[2,256,512]{2,1,0:T(8,128)S(1)}, f32[2,256,512]{2,1,0:T(8,128)S(1)}, u32[]{:S(2)}, u32[]{:S(2)}) %collective-permute-start.1) | collective-permute-done | bytes 1048608 | tf_op jit(solution)/shard_map/while/body/eval_jaxpr/ppermute | solution.py:16
  (289 shorter events, 247.5 us)
Async XLA Ops:
  0.6 10.7 copy-start.18
  2.6 14.6 %collective-permute-start.2 = (bf16[2,256,512]{2,1,0:T(8,128)(2,1)}, bf16[2,256,512]{2,1,0:T(8,128)(2,1)}, u32[]{:S(2)}, u32[]{:S(2)}) collective-permute-start(bf16[2,256,512]{2,1,0:T(8,128)(2,1)} %pad_maximum_fusion.2), channel_id=1, source_target_pairs={{32,0},{36,4},{40,8},{44,12},{48,16},{52,20},{56,24},{60,28},{64,3... | collective-permute-start | bytes 1572872 | tf_op jit(solution)/shard_map/ppermute | solution.py:16
  22.7 18.5 %collective-permute-start = (bf16[2,256,512]{2,1,0:T(8,128)(2,1)}, bf16[2,256,512]{2,1,0:T(8,128)(2,1)S(1)}, u32[]{:S(2)}, u32[]{:S(2)}) collective-permute-start(bf16[2,256,512]{2,1,0:T(8,128)(2,1)} %get-tuple-element.288), channel_id=1, source_target_pairs={{124,0},{0,4},{4,8},{8,12},{12,16},{16,20},{20,24},{24,28},{28,32}... | collective-permute-start | bytes 1572872 | tf_op jit(solution)/shard_map/while/body/eval_jaxpr/ppermute | solution.py:16
  42.9 16.6 %collective-permute-start = (bf16[2,256,512]{2,1,0:T(8,128)(2,1)}, bf16[2,256,512]{2,1,0:T(8,128)(2,1)S(1)}, u32[]{:S(2)}, u32[]{:S(2)}) collective-permute-start(bf16[2,256,512]{2,1,0:T(8,128)(2,1)} %get-tuple-element.288), channel_id=1, source_target_pairs={{124,0},{0,4},{4,8},{8,12},{12,16},{16,20},{20,24},{24,28},{28,32}... | collective-permute-start | bytes 1572872 | tf_op jit(solution)/shard_map/while/body/eval_jaxpr/ppermute | solution.py:16
  61.2 15.7 %collective-permute-start = (bf16[2,256,512]{2,1,0:T(8,128)(2,1)}, bf16[2,256,512]{2,1,0:T(8,128)(2,1)S(1)}, u32[]{:S(2)}, u32[]{:S(2)}) collective-permute-start(bf16[2,256,512]{2,1,0:T(8,128)(2,1)} %get-tuple-element.288), channel_id=1, source_target_pairs={{124,0},{0,4},{4,8},{8,12},{12,16},{16,20},{20,24},{24,28},{28,32}... | collective-permute-start | bytes 1572872 | tf_op jit(solution)/shard_map/while/body/eval_jaxpr/ppermute | solution.py:16
  78.5 14.7 %collective-permute-start = (bf16[2,256,512]{2,1,0:T(8,128)(2,1)}, bf16[2,256,512]{2,1,0:T(8,128)(2,1)S(1)}, u32[]{:S(2)}, u32[]{:S(2)}) collective-permute-start(bf16[2,256,512]{2,1,0:T(8,128)(2,1)} %get-tuple-element.288), channel_id=1, source_target_pairs={{124,0},{0,4},{4,8},{8,12},{12,16},{16,20},{20,24},{24,28},{28,32}... | collective-permute-start | bytes 1572872 | tf_op jit(solution)/shard_map/while/body/eval_jaxpr/ppermute | solution.py:16
  94.8 13.8 %collective-permute-start = (bf16[2,256,512]{2,1,0:T(8,128)(2,1)}, bf16[2,256,512]{2,1,0:T(8,128)(2,1)S(1)}, u32[]{:S(2)}, u32[]{:S(2)}) collective-permute-start(bf16[2,256,512]{2,1,0:T(8,128)(2,1)} %get-tuple-element.288), channel_id=1, source_target_pairs={{124,0},{0,4},{4,8},{8,12},{12,16},{16,20},{20,24},{24,28},{28,32}... | collective-permute-start | bytes 1572872 | tf_op jit(solution)/shard_map/while/body/eval_jaxpr/ppermute | solution.py:16
  110.3 13.6 %collective-permute-start = (bf16[2,256,512]{2,1,0:T(8,128)(2,1)}, bf16[2,256,512]{2,1,0:T(8,128)(2,1)S(1)}, u32[]{:S(2)}, u32[]{:S(2)}) collective-permute-start(bf16[2,256,512]{2,1,0:T(8,128)(2,1)} %get-tuple-element.288), channel_id=1, source_target_pairs={{124,0},{0,4},{4,8},{8,12},{12,16},{16,20},{20,24},{24,28},{28,32}... | collective-permute-start | bytes 1572872 | tf_op jit(solution)/shard_map/while/body/eval_jaxpr/ppermute | solution.py:16
  125.5 13.6 %collective-permute-start = (bf16[2,256,512]{2,1,0:T(8,128)(2,1)}, bf16[2,256,512]{2,1,0:T(8,128)(2,1)S(1)}, u32[]{:S(2)}, u32[]{:S(2)}) collective-permute-start(bf16[2,256,512]{2,1,0:T(8,128)(2,1)} %get-tuple-element.288), channel_id=1, source_target_pairs={{124,0},{0,4},{4,8},{8,12},{12,16},{16,20},{20,24},{24,28},{28,32}... | collective-permute-start | bytes 1572872 | tf_op jit(solution)/shard_map/while/body/eval_jaxpr/ppermute | solution.py:16
  140.7 13.7 %collective-permute-start = (bf16[2,256,512]{2,1,0:T(8,128)(2,1)}, bf16[2,256,512]{2,1,0:T(8,128)(2,1)S(1)}, u32[]{:S(2)}, u32[]{:S(2)}) collective-permute-start(bf16[2,256,512]{2,1,0:T(8,128)(2,1)} %get-tuple-element.288), channel_id=1, source_target_pairs={{124,0},{0,4},{4,8},{8,12},{12,16},{16,20},{20,24},{24,28},{28,32}... | collective-permute-start | bytes 1572872 | tf_op jit(solution)/shard_map/while/body/eval_jaxpr/ppermute | solution.py:16
  156.1 14.8 %collective-permute-start = (bf16[2,256,512]{2,1,0:T(8,128)(2,1)}, bf16[2,256,512]{2,1,0:T(8,128)(2,1)S(1)}, u32[]{:S(2)}, u32[]{:S(2)}) collective-permute-start(bf16[2,256,512]{2,1,0:T(8,128)(2,1)} %get-tuple-element.288), channel_id=1, source_target_pairs={{124,0},{0,4},{4,8},{8,12},{12,16},{16,20},{20,24},{24,28},{28,32}... | collective-permute-start | bytes 1572872 | tf_op jit(solution)/shard_map/while/body/eval_jaxpr/ppermute | solution.py:16
  172.5 15.9 %collective-permute-start = (bf16[2,256,512]{2,1,0:T(8,128)(2,1)}, bf16[2,256,512]{2,1,0:T(8,128)(2,1)S(1)}, u32[]{:S(2)}, u32[]{:S(2)}) collective-permute-start(bf16[2,256,512]{2,1,0:T(8,128)(2,1)} %get-tuple-element.288), channel_id=1, source_target_pairs={{124,0},{0,4},{4,8},{8,12},{12,16},{16,20},{20,24},{24,28},{28,32}... | collective-permute-start | bytes 1572872 | tf_op jit(solution)/shard_map/while/body/eval_jaxpr/ppermute | solution.py:16
  190.0 17.0 %collective-permute-start = (bf16[2,256,512]{2,1,0:T(8,128)(2,1)}, bf16[2,256,512]{2,1,0:T(8,128)(2,1)S(1)}, u32[]{:S(2)}, u32[]{:S(2)}) collective-permute-start(bf16[2,256,512]{2,1,0:T(8,128)(2,1)} %get-tuple-element.288), channel_id=1, source_target_pairs={{124,0},{0,4},{4,8},{8,12},{12,16},{16,20},{20,24},{24,28},{28,32}... | collective-permute-start | bytes 1572872 | tf_op jit(solution)/shard_map/while/body/eval_jaxpr/ppermute | solution.py:16
  208.6 18.1 %collective-permute-start = (bf16[2,256,512]{2,1,0:T(8,128)(2,1)}, bf16[2,256,512]{2,1,0:T(8,128)(2,1)S(1)}, u32[]{:S(2)}, u32[]{:S(2)}) collective-permute-start(bf16[2,256,512]{2,1,0:T(8,128)(2,1)} %get-tuple-element.288), channel_id=1, source_target_pairs={{124,0},{0,4},{4,8},{8,12},{12,16},{16,20},{20,24},{24,28},{28,32}... | collective-permute-start | bytes 1572872 | tf_op jit(solution)/shard_map/while/body/eval_jaxpr/ppermute | solution.py:16
  228.3 19.2 %collective-permute-start = (bf16[2,256,512]{2,1,0:T(8,128)(2,1)}, bf16[2,256,512]{2,1,0:T(8,128)(2,1)S(1)}, u32[]{:S(2)}, u32[]{:S(2)}) collective-permute-start(bf16[2,256,512]{2,1,0:T(8,128)(2,1)} %get-tuple-element.288), channel_id=1, source_target_pairs={{124,0},{0,4},{4,8},{8,12},{12,16},{16,20},{20,24},{24,28},{28,32}... | collective-permute-start | bytes 1572872 | tf_op jit(solution)/shard_map/while/body/eval_jaxpr/ppermute | solution.py:16
  249.1 18.4 %collective-permute-start = (bf16[2,256,512]{2,1,0:T(8,128)(2,1)}, bf16[2,256,512]{2,1,0:T(8,128)(2,1)S(1)}, u32[]{:S(2)}, u32[]{:S(2)}) collective-permute-start(bf16[2,256,512]{2,1,0:T(8,128)(2,1)} %get-tuple-element.288), channel_id=1, source_target_pairs={{124,0},{0,4},{4,8},{8,12},{12,16},{16,20},{20,24},{24,28},{28,32}... | collective-permute-start | bytes 1572872 | tf_op jit(solution)/shard_map/while/body/eval_jaxpr/ppermute | solution.py:16
  269.1 17.5 %collective-permute-start = (bf16[2,256,512]{2,1,0:T(8,128)(2,1)}, bf16[2,256,512]{2,1,0:T(8,128)(2,1)S(1)}, u32[]{:S(2)}, u32[]{:S(2)}) collective-permute-start(bf16[2,256,512]{2,1,0:T(8,128)(2,1)} %get-tuple-element.288), channel_id=1, source_target_pairs={{124,0},{0,4},{4,8},{8,12},{12,16},{16,20},{20,24},{24,28},{28,32}... | collective-permute-start | bytes 1572872 | tf_op jit(solution)/shard_map/while/body/eval_jaxpr/ppermute | solution.py:16
  288.3 13.6 %collective-permute-start = (bf16[2,256,512]{2,1,0:T(8,128)(2,1)}, bf16[2,256,512]{2,1,0:T(8,128)(2,1)S(1)}, u32[]{:S(2)}, u32[]{:S(2)}) collective-permute-start(bf16[2,256,512]{2,1,0:T(8,128)(2,1)} %get-tuple-element.288), channel_id=1, source_target_pairs={{124,0},{0,4},{4,8},{8,12},{12,16},{16,20},{20,24},{24,28},{28,32}... | collective-permute-start | bytes 1572872 | tf_op jit(solution)/shard_map/while/body/eval_jaxpr/ppermute | solution.py:16
  356.3 4.9 copy-start.13
  366.0 9.2 slice-start.6
  366.0 9.2 slice-start.12
  366.0 9.2 slice-start.7
  366.0 9.2 slice-start.13
  390.2 4.9 copy-start.12
  399.9 9.2 slice-start.8
  399.9 9.2 slice-start.14
  399.9 9.2 slice-start.9
  399.9 9.2 slice-start.15
  403.6 4.1 copy-start.8
  424.4 4.9 copy-start.11
  434.0 9.2 slice-start.10
  434.0 9.2 slice-start.16
  434.0 9.2 slice-start.11
  434.0 9.2 slice-start.17
  437.7 4.1 copy-start.9
  437.7 4.1 copy-start.15
  487.3 5.4 copy-start.10
  496.6 8.4 copy-start.14
  501.4 7.4 slice-start.4
  501.4 7.4 slice-start.18
  501.4 7.4 slice-start.5
  501.4 7.8 slice-start.19
  588.4 8.0 copy-start.27
  607.1 5.9 slice-start
  665.9 24.6 %collective-permute-start.1 = (f32[2,256,512]{2,1,0:T(8,128)S(1)}, f32[2,256,512]{2,1,0:T(8,128)S(1)}, u32[]{:S(2)}, u32[]{:S(2)}) collective-permute-start(f32[2,256,512]{2,1,0:T(8,128)S(1)} %get-tuple-element.308), channel_id=1, source_target_pairs={{4,0},{8,4},{12,8},{16,12},{20,16},{24,20},{28,24},{32,28},{36,32}... | collective-permute-start | bytes 3145736 | tf_op jit(solution)/shard_map/while/body/eval_jaxpr/ppermute | solution.py:16
  691.9 28.1 %collective-permute-start.1 = (f32[2,256,512]{2,1,0:T(8,128)S(1)}, f32[2,256,512]{2,1,0:T(8,128)S(1)}, u32[]{:S(2)}, u32[]{:S(2)}) collective-permute-start(f32[2,256,512]{2,1,0:T(8,128)S(1)} %get-tuple-element.308), channel_id=1, source_target_pairs={{4,0},{8,4},{12,8},{16,12},{20,16},{24,20},{28,24},{32,28},{36,32}... | collective-permute-start | bytes 3145736 | tf_op jit(solution)/shard_map/while/body/eval_jaxpr/ppermute | solution.py:16
  721.4 27.9 %collective-permute-start.1 = (f32[2,256,512]{2,1,0:T(8,128)S(1)}, f32[2,256,512]{2,1,0:T(8,128)S(1)}, u32[]{:S(2)}, u32[]{:S(2)}) collective-permute-start(f32[2,256,512]{2,1,0:T(8,128)S(1)} %get-tuple-element.308), channel_id=1, source_target_pairs={{4,0},{8,4},{12,8},{16,12},{20,16},{24,20},{28,24},{32,28},{36,32}... | collective-permute-start | bytes 3145736 | tf_op jit(solution)/shard_map/while/body/eval_jaxpr/ppermute | solution.py:16
  750.8 27.0 %collective-permute-start.1 = (f32[2,256,512]{2,1,0:T(8,128)S(1)}, f32[2,256,512]{2,1,0:T(8,128)S(1)}, u32[]{:S(2)}, u32[]{:S(2)}) collective-permute-start(f32[2,256,512]{2,1,0:T(8,128)S(1)} %get-tuple-element.308), channel_id=1, source_target_pairs={{4,0},{8,4},{12,8},{16,12},{20,16},{24,20},{28,24},{32,28},{36,32}... | collective-permute-start | bytes 3145736 | tf_op jit(solution)/shard_map/while/body/eval_jaxpr/ppermute | solution.py:16
  779.2 26.1 %collective-permute-start.1 = (f32[2,256,512]{2,1,0:T(8,128)S(1)}, f32[2,256,512]{2,1,0:T(8,128)S(1)}, u32[]{:S(2)}, u32[]{:S(2)}) collective-permute-start(f32[2,256,512]{2,1,0:T(8,128)S(1)} %get-tuple-element.308), channel_id=1, source_target_pairs={{4,0},{8,4},{12,8},{16,12},{20,16},{24,20},{28,24},{32,28},{36,32}... | collective-permute-start | bytes 3145736 | tf_op jit(solution)/shard_map/while/body/eval_jaxpr/ppermute | solution.py:16
  806.7 25.2 %collective-permute-start.1 = (f32[2,256,512]{2,1,0:T(8,128)S(1)}, f32[2,256,512]{2,1,0:T(8,128)S(1)}, u32[]{:S(2)}, u32[]{:S(2)}) collective-permute-start(f32[2,256,512]{2,1,0:T(8,128)S(1)} %get-tuple-element.308), channel_id=1, source_target_pairs={{4,0},{8,4},{12,8},{16,12},{20,16},{24,20},{28,24},{32,28},{36,32}... | collective-permute-start | bytes 3145736 | tf_op jit(solution)/shard_map/while/body/eval_jaxpr/ppermute | solution.py:16
  833.3 24.2 %collective-permute-start.1 = (f32[2,256,512]{2,1,0:T(8,128)S(1)}, f32[2,256,512]{2,1,0:T(8,128)S(1)}, u32[]{:S(2)}, u32[]{:S(2)}) collective-permute-start(f32[2,256,512]{2,1,0:T(8,128)S(1)} %get-tuple-element.308), channel_id=1, source_target_pairs={{4,0},{8,4},{12,8},{16,12},{20,16},{24,20},{28,24},{32,28},{36,32}... | collective-permute-start | bytes 3145736 | tf_op jit(solution)/shard_map/while/body/eval_jaxpr/ppermute | solution.py:16
  859.0 23.3 %collective-permute-start.1 = (f32[2,256,512]{2,1,0:T(8,128)S(1)}, f32[2,256,512]{2,1,0:T(8,128)S(1)}, u32[]{:S(2)}, u32[]{:S(2)}) collective-permute-start(f32[2,256,512]{2,1,0:T(8,128)S(1)} %get-tuple-element.308), channel_id=1, source_target_pairs={{4,0},{8,4},{12,8},{16,12},{20,16},{24,20},{28,24},{32,28},{36,32}... | collective-permute-start | bytes 3145736 | tf_op jit(solution)/shard_map/while/body/eval_jaxpr/ppermute | solution.py:16
  883.8 22.4 %collective-permute-start.1 = (f32[2,256,512]{2,1,0:T(8,128)S(1)}, f32[2,256,512]{2,1,0:T(8,128)S(1)}, u32[]{:S(2)}, u32[]{:S(2)}) collective-permute-start(f32[2,256,512]{2,1,0:T(8,128)S(1)} %get-tuple-element.308), channel_id=1, source_target_pairs={{4,0},{8,4},{12,8},{16,12},{20,16},{24,20},{28,24},{32,28},{36,32}... | collective-permute-start | bytes 3145736 | tf_op jit(solution)/shard_map/while/body/eval_jaxpr/ppermute | solution.py:16
  907.6 21.9 %collective-permute-start.1 = (f32[2,256,512]{2,1,0:T(8,128)S(1)}, f32[2,256,512]{2,1,0:T(8,128)S(1)}, u32[]{:S(2)}, u32[]{:S(2)}) collective-permute-start(f32[2,256,512]{2,1,0:T(8,128)S(1)} %get-tuple-element.308), channel_id=1, source_target_pairs={{4,0},{8,4},{12,8},{16,12},{20,16},{24,20},{28,24},{32,28},{36,32}... | collective-permute-start | bytes 3145736 | tf_op jit(solution)/shard_map/while/body/eval_jaxpr/ppermute | solution.py:16
  930.9 21.9 %collective-permute-start.1 = (f32[2,256,512]{2,1,0:T(8,128)S(1)}, f32[2,256,512]{2,1,0:T(8,128)S(1)}, u32[]{:S(2)}, u32[]{:S(2)}) collective-permute-start(f32[2,256,512]{2,1,0:T(8,128)S(1)} %get-tuple-element.308), channel_id=1, source_target_pairs={{4,0},{8,4},{12,8},{16,12},{20,16},{24,20},{28,24},{32,28},{36,32}... | collective-permute-start | bytes 3145736 | tf_op jit(solution)/shard_map/while/body/eval_jaxpr/ppermute | solution.py:16
  954.3 21.9 %collective-permute-start.1 = (f32[2,256,512]{2,1,0:T(8,128)S(1)}, f32[2,256,512]{2,1,0:T(8,128)S(1)}, u32[]{:S(2)}, u32[]{:S(2)}) collective-permute-start(f32[2,256,512]{2,1,0:T(8,128)S(1)} %get-tuple-element.308), channel_id=1, source_target_pairs={{4,0},{8,4},{12,8},{16,12},{20,16},{24,20},{28,24},{32,28},{36,32}... | collective-permute-start | bytes 3145736 | tf_op jit(solution)/shard_map/while/body/eval_jaxpr/ppermute | solution.py:16
  977.6 22.3 %collective-permute-start.1 = (f32[2,256,512]{2,1,0:T(8,128)S(1)}, f32[2,256,512]{2,1,0:T(8,128)S(1)}, u32[]{:S(2)}, u32[]{:S(2)}) collective-permute-start(f32[2,256,512]{2,1,0:T(8,128)S(1)} %get-tuple-element.308), channel_id=1, source_target_pairs={{4,0},{8,4},{12,8},{16,12},{20,16},{24,20},{28,24},{32,28},{36,32}... | collective-permute-start | bytes 3145736 | tf_op jit(solution)/shard_map/while/body/eval_jaxpr/ppermute | solution.py:16
  1001.3 23.4 %collective-permute-start.1 = (f32[2,256,512]{2,1,0:T(8,128)S(1)}, f32[2,256,512]{2,1,0:T(8,128)S(1)}, u32[]{:S(2)}, u32[]{:S(2)}) collective-permute-start(f32[2,256,512]{2,1,0:T(8,128)S(1)} %get-tuple-element.308), channel_id=1, source_target_pairs={{4,0},{8,4},{12,8},{16,12},{20,16},{24,20},{28,24},{32,28},{36,32}... | collective-permute-start | bytes 3145736 | tf_op jit(solution)/shard_map/while/body/eval_jaxpr/ppermute | solution.py:16
  1026.1 24.5 %collective-permute-start.1 = (f32[2,256,512]{2,1,0:T(8,128)S(1)}, f32[2,256,512]{2,1,0:T(8,128)S(1)}, u32[]{:S(2)}, u32[]{:S(2)}) collective-permute-start(f32[2,256,512]{2,1,0:T(8,128)S(1)} %get-tuple-element.308), channel_id=1, source_target_pairs={{4,0},{8,4},{12,8},{16,12},{20,16},{24,20},{28,24},{32,28},{36,32}... | collective-permute-start | bytes 3145736 | tf_op jit(solution)/shard_map/while/body/eval_jaxpr/ppermute | solution.py:16
  1052.0 19.1 %collective-permute-start.1 = (f32[2,256,512]{2,1,0:T(8,128)S(1)}, f32[2,256,512]{2,1,0:T(8,128)S(1)}, u32[]{:S(2)}, u32[]{:S(2)}) collective-permute-start(f32[2,256,512]{2,1,0:T(8,128)S(1)} %get-tuple-element.308), channel_id=1, source_target_pairs={{4,0},{8,4},{12,8},{16,12},{20,16},{24,20},{28,24},{32,28},{36,32}... | collective-permute-start | bytes 3145736 | tf_op jit(solution)/shard_map/while/body/eval_jaxpr/ppermute | solution.py:16
  1072.6 4.9 copy-start.19
  1072.6 4.9 copy-start.20
  1072.6 4.9 copy-start.21
  1073.4 10.9 %collective-permute-start.3 = (bf16[2,256,512]{2,1,0:T(8,128)(2,1)}, bf16[2,256,512]{2,1,0:T(8,128)(2,1)}, u32[]{:S(2)}, u32[]{:S(2)}) collective-permute-start(bf16[2,256,512]{2,1,0:T(8,128)(2,1)} %convert_element_type.84), channel_id=1, source_target_pairs={{96,0},{100,4},{104,8},{108,12},{112,16},{116,20},{120,24},{124,28... | collective-permute-start | bytes 1572872 | tf_op jit(solution)/shard_map/ppermute | solution.py:16
  (20 other events, 55.0 us)
where the time goes:
time: 1100 us; the launch traced here: 1090 us
  waiting for transfers between devices  536 us (49%)
  local copies, waits for them, and re-layouts  211 us (19%)
  matrix products  114 us (10%)
  starting transfers between devices  107 us (10%)
  blocking collectives  63.8 us (6%)
  other arithmetic  52.3 us (5%)
    ppermute x34, waiting for transfers between devices, passed_along(): return lax.ppermute(block, axis, route)  536 us
    ppermute x34, starting transfers between devices, passed_along(): return lax.ppermute(block, axis, route)  107 us
    psum x1, blocking collectives, body(): scale_total = lax.psum(jnp.stack(scale_parts), ('ctx', 'batch'))  63.8 us
    another operation x6, local copies, waits for them, and re-layouts, body(): jnp.stack(placed_parts)  24.6 us
    dot_general x4, matrix products, body(): jnp.einsum('sw,csx->cwx', chooser, both_parts, precision=lax.Precision.HI...  24.4 us
    slice x1, local copies, waits for them, and re-layouts, body(): blocks_all[0, :, :, group_id]  23.1 us
    add x16, other arithmetic, chain_turn(): moved + lax.dynamic_index_in_dim(grads_window, turn_no, 0, keepdims=False)  22.9 us
  transfers between devices with their start and end apart: 34, of which 34 were waited for; matrix products, arithmetic and copies ran while one was open for 2% of the time, Pallas kernels for 0%

commit v1 on v0

--- a/solution.py
+++ b/solution.py
@@ -113,7 +113,8 @@
     )
     key_grad = summed[0].reshape(1, tokens, KV_HEADS * HD).astype(jnp.bfloat16)
     value_grad = summed[1].reshape(1, tokens, KV_HEADS * HD).astype(jnp.bfloat16)
-    scale_total = lax.psum(jnp.stack(scale_parts), ("ctx", "batch"))
+    inner = lax.psum(jnp.stack(scale_parts), "ctx")
+    scale_total = lax.psum(inner, "batch")
     tau_grad = scale_total.reshape(HEADS) / math.sqrt(lax.axis_size("batch") * ctx_size * tokens)
     return (attended, query_grad, key_grad, value_grad, tau_grad)
 

time: 1100 us -> 1110 us (level)
  blocking collectives: 63.8 us -> 84.2 us
    psum x1 -> x2, blocking collectives: 63.8 us -> 84.2 us  [the longest x1 76.8 us: body(): inner = lax.psum(jnp.stack(scale_parts), 'ctx')]
where the time goes in v1:
time: 1110 us
  waiting for transfers between devices  534 us (48%)
  local copies, waits for them, and re-layouts  212 us (19%)
  matrix products  115 us (10%)
  starting transfers between devices  108 us (10%)
  blocking collectives  84.2 us (8%)
  other arithmetic  50.9 us (5%)
    ppermute x34, waiting for transfers between devices, passed_along(): return lax.ppermute(block, axis, route)  534 us
    ppermute x34, starting transfers between devices, passed_along(): return lax.ppermute(block, axis, route)  108 us
    psum x1, blocking collectives, body(): inner = lax.psum(jnp.stack(scale_parts), 'ctx')  76.8 us
    dot_general x4, matrix products, body(): jnp.einsum('sw,csx->cwx', chooser, both_parts, precision=lax.Precision.HI...  25.9 us
    another operation x6, local copies, waits for them, and re-layouts, body(): jnp.stack(placed_parts)  24.5 us
    slice x1, local copies, waits for them, and re-layouts, body(): blocks_all[0, :, :, group_id]  23.5 us
    add x16, other arithmetic, chain_turn(): moved + lax.dynamic_index_in_dim(grads_window, turn_no, 0, keepdims=False)  22.9 us
  transfers between devices with their start and end apart: 34, of which 34 were waited for; matrix products, arithmetic and copies ran while one was open for 2% of the time, Pallas kernels for 0%

profile of v1, /device:TPU:0, one launch (start us, length us, event | category | flops | bytes accessed | tf_op | source)
XLA Modules:
  0.0 1105.4 jit_solution(8288937326459912877)
XLA Ops:
  17.2 5.5 dynamic_update_slice.10
  22.7 281.0 %while.30 = (s32[]{:T(128)}, bf16[2,256,512]{2,1,0:T(8,128)(2,1)}, bf16[2,17,256,512]{3,2,0,1:T(8,128)(2,1)}, s32[]{:T(128)}, s32[]{:T(128)}, /*index=5*/s32[]{:T(128)}, s32[]{:T(128)}) while((s32[]{:T(128)}, bf16[2,256,512]{2,1,0:T(8,128)(2,1)}, bf16[2,17,256,512]{3,2,0,1:T(8,128)(2,1)}, s32[]{:T(128)}, s32[]{:T(128)}, /*index=5*/s32[]{:T(128)}, ...), condition=%wide.region_1.0_spmd, body=%wide.region_0.0_spmd.sunk | while | flops 6 | bytes 4194471 | solution.py:43
  24.6 16.6 %collective-permute-done = bf16[2,256,512]{2,1,0:T(8,128)(2,1)S(1)} collective-permute-done((bf16[2,256,512]{2,1,0:T(8,128)(2,1)}, bf16[2,256,512]{2,1,0:T(8,128)(2,1)S(1)}, u32[]{:S(2)}, u32[]{:S(2)}) %collective-permute-start) | collective-permute-done | bytes 524320 | tf_op jit(solution)/shard_map/while/body/eval_jaxpr/ppermute | solution.py:16
  42.9 16.6 %collective-permute-done = bf16[2,256,512]{2,1,0:T(8,128)(2,1)S(1)} collective-permute-done((bf16[2,256,512]{2,1,0:T(8,128)(2,1)}, bf16[2,256,512]{2,1,0:T(8,128)(2,1)S(1)}, u32[]{:S(2)}, u32[]{:S(2)}) %collective-permute-start) | collective-permute-done | bytes 524320 | tf_op jit(solution)/shard_map/while/body/eval_jaxpr/ppermute | solution.py:16
  61.2 15.7 %collective-permute-done = bf16[2,256,512]{2,1,0:T(8,128)(2,1)S(1)} collective-permute-done((bf16[2,256,512]{2,1,0:T(8,128)(2,1)}, bf16[2,256,512]{2,1,0:T(8,128)(2,1)S(1)}, u32[]{:S(2)}, u32[]{:S(2)}) %collective-permute-start) | collective-permute-done | bytes 524320 | tf_op jit(solution)/shard_map/while/body/eval_jaxpr/ppermute | solution.py:16
  78.5 14.7 %collective-permute-done = bf16[2,256,512]{2,1,0:T(8,128)(2,1)S(1)} collective-permute-done((bf16[2,256,512]{2,1,0:T(8,128)(2,1)}, bf16[2,256,512]{2,1,0:T(8,128)(2,1)S(1)}, u32[]{:S(2)}, u32[]{:S(2)}) %collective-permute-start) | collective-permute-done | bytes 524320 | tf_op jit(solution)/shard_map/while/body/eval_jaxpr/ppermute | solution.py:16
  94.8 13.8 %collective-permute-done = bf16[2,256,512]{2,1,0:T(8,128)(2,1)S(1)} collective-permute-done((bf16[2,256,512]{2,1,0:T(8,128)(2,1)}, bf16[2,256,512]{2,1,0:T(8,128)(2,1)S(1)}, u32[]{:S(2)}, u32[]{:S(2)}) %collective-permute-start) | collective-permute-done | bytes 524320 | tf_op jit(solution)/shard_map/while/body/eval_jaxpr/ppermute | solution.py:16
  110.3 13.6 %collective-permute-done = bf16[2,256,512]{2,1,0:T(8,128)(2,1)S(1)} collective-permute-done((bf16[2,256,512]{2,1,0:T(8,128)(2,1)}, bf16[2,256,512]{2,1,0:T(8,128)(2,1)S(1)}, u32[]{:S(2)}, u32[]{:S(2)}) %collective-permute-start) | collective-permute-done | bytes 524320 | tf_op jit(solution)/shard_map/while/body/eval_jaxpr/ppermute | solution.py:16
  125.6 13.6 %collective-permute-done = bf16[2,256,512]{2,1,0:T(8,128)(2,1)S(1)} collective-permute-done((bf16[2,256,512]{2,1,0:T(8,128)(2,1)}, bf16[2,256,512]{2,1,0:T(8,128)(2,1)S(1)}, u32[]{:S(2)}, u32[]{:S(2)}) %collective-permute-start) | collective-permute-done | bytes 524320 | tf_op jit(solution)/shard_map/while/body/eval_jaxpr/ppermute | solution.py:16
  140.9 13.7 %collective-permute-done = bf16[2,256,512]{2,1,0:T(8,128)(2,1)S(1)} collective-permute-done((bf16[2,256,512]{2,1,0:T(8,128)(2,1)}, bf16[2,256,512]{2,1,0:T(8,128)(2,1)S(1)}, u32[]{:S(2)}, u32[]{:S(2)}) %collective-permute-start) | collective-permute-done | bytes 524320 | tf_op jit(solution)/shard_map/while/body/eval_jaxpr/ppermute | solution.py:16
  156.2 14.8 %collective-permute-done = bf16[2,256,512]{2,1,0:T(8,128)(2,1)S(1)} collective-permute-done((bf16[2,256,512]{2,1,0:T(8,128)(2,1)}, bf16[2,256,512]{2,1,0:T(8,128)(2,1)S(1)}, u32[]{:S(2)}, u32[]{:S(2)}) %collective-permute-start) | collective-permute-done | bytes 524320 | tf_op jit(solution)/shard_map/while/body/eval_jaxpr/ppermute | solution.py:16
  172.6 15.8 %collective-permute-done = bf16[2,256,512]{2,1,0:T(8,128)(2,1)S(1)} collective-permute-done((bf16[2,256,512]{2,1,0:T(8,128)(2,1)}, bf16[2,256,512]{2,1,0:T(8,128)(2,1)S(1)}, u32[]{:S(2)}, u32[]{:S(2)}) %collective-permute-start) | collective-permute-done | bytes 524320 | tf_op jit(solution)/shard_map/while/body/eval_jaxpr/ppermute | solution.py:16
  190.1 16.9 %collective-permute-done = bf16[2,256,512]{2,1,0:T(8,128)(2,1)S(1)} collective-permute-done((bf16[2,256,512]{2,1,0:T(8,128)(2,1)}, bf16[2,256,512]{2,1,0:T(8,128)(2,1)S(1)}, u32[]{:S(2)}, u32[]{:S(2)}) %collective-permute-start) | collective-permute-done | bytes 524320 | tf_op jit(solution)/shard_map/while/body/eval_jaxpr/ppermute | solution.py:16
  208.7 18.1 %collective-permute-done = bf16[2,256,512]{2,1,0:T(8,128)(2,1)S(1)} collective-permute-done((bf16[2,256,512]{2,1,0:T(8,128)(2,1)}, bf16[2,256,512]{2,1,0:T(8,128)(2,1)S(1)}, u32[]{:S(2)}, u32[]{:S(2)}) %collective-permute-start) | collective-permute-done | bytes 524320 | tf_op jit(solution)/shard_map/while/body/eval_jaxpr/ppermute | solution.py:16
  228.4 19.2 %collective-permute-done = bf16[2,256,512]{2,1,0:T(8,128)(2,1)S(1)} collective-permute-done((bf16[2,256,512]{2,1,0:T(8,128)(2,1)}, bf16[2,256,512]{2,1,0:T(8,128)(2,1)S(1)}, u32[]{:S(2)}, u32[]{:S(2)}) %collective-permute-start) | collective-permute-done | bytes 524320 | tf_op jit(solution)/shard_map/while/body/eval_jaxpr/ppermute | solution.py:16
  249.3 18.4 %collective-permute-done = bf16[2,256,512]{2,1,0:T(8,128)(2,1)S(1)} collective-permute-done((bf16[2,256,512]{2,1,0:T(8,128)(2,1)}, bf16[2,256,512]{2,1,0:T(8,128)(2,1)S(1)}, u32[]{:S(2)}, u32[]{:S(2)}) %collective-permute-start) | collective-permute-done | bytes 524320 | tf_op jit(solution)/shard_map/while/body/eval_jaxpr/ppermute | solution.py:16
  269.3 17.5 %collective-permute-done = bf16[2,256,512]{2,1,0:T(8,128)(2,1)S(1)} collective-permute-done((bf16[2,256,512]{2,1,0:T(8,128)(2,1)}, bf16[2,256,512]{2,1,0:T(8,128)(2,1)S(1)}, u32[]{:S(2)}, u32[]{:S(2)}) %collective-permute-start) | collective-permute-done | bytes 524320 | tf_op jit(solution)/shard_map/while/body/eval_jaxpr/ppermute | solution.py:16
  288.5 13.6 %collective-permute-done = bf16[2,256,512]{2,1,0:T(8,128)(2,1)S(1)} collective-permute-done((bf16[2,256,512]{2,1,0:T(8,128)(2,1)}, bf16[2,256,512]{2,1,0:T(8,128)(2,1)S(1)}, u32[]{:S(2)}, u32[]{:S(2)}) %collective-permute-start) | collective-permute-done | bytes 524320 | tf_op jit(solution)/shard_map/while/body/eval_jaxpr/ppermute | solution.py:16
  303.8 8.0 copy.85
  311.8 13.4 %reshape.174 = bf16[2,34,128,4,128]{4,3,2,1,0:T(4,128)(2,1)} reshape(bf16[2,17,256,512]{3,2,1,0:T(8,128)(2,1)} %copy.85) | data formatting | bytes 17825792 | tf_op jit(solution)/shard_map/reshape | solution.py:44
  325.1 23.5 %fusion.82 = (bf16[1,34,128,1,128]{4,3,2,1,0:T(2,128)(2,1)S(1)}, bf16[1,34,128,1,128]{4,3,2,1,0:T(2,128)(2,1)}, bf16[1,34,128,1,128]{4,3,2,1,0:T(2,128)(2,1)}, b...) fusion(bf16[2,34,128,4,128]{4,3,2,1,0:T(4,128)(2,1)} %reshape.174), kind=kLoop, calls=%fused_computation.196 | loop fusion | bytes 17825792 | tf_op jit(solution)/shard_map/slice | solution.py:59
  357.0 4.9 fusion.57
  460.3 6.5 convolution_bitcast_fusion.2
  475.4 6.5 convolution_bitcast_fusion.1
  490.6 6.5 convolution_bitcast_fusion
  523.0 76.8 %psum.14 = f32[4,4]{1,0:T(4,128)S(1)} all-reduce(f32[4,4]{1,0:T(4,128)S(1)} %pad_maximum_fusion.3), channel_id=1, replica_groups=mesh['ctx'=32,'batch'=4] {'ctx'}, use_global_device_ids=true, to_apply=%region_20.22 | all-reduce | flops 16 | bytes 128 | tf_op jit(solution)/shard_map/psum | solution.py:116
  599.8 7.4 psum.15
  609.4 5.2 convolution_bitcast_fusion.11
  617.4 6.5 convolution_bitcast_fusion.3
  635.8 6.7 copy.256
  642.4 19.9 %copy.128 = f32[17,2,2,128,4,128]{5,4,3,2,1,0:T(4,128)} copy(f32[17,2,2,128,4,128]{5,3,2,0,1,4:T(8,128)S(1)} %bitcast.371) | data formatting | bytes 35651584 | tf_op jit(solution)/shard_map/transpose | solution.py:104
  662.3 21.9 %reshape.183 = f32[17,2,256,512]{3,2,1,0:T(8,128)} reshape(f32[17,2,2,128,4,128]{5,4,3,2,1,0:T(4,128)} %copy.128) | data formatting | bytes 35651584 | tf_op jit(solution)/shard_map/reshape | solution.py:104
  686.7 404.6 %while.31 = (s32[]{:T(128)}, f32[2,256,512]{2,1,0:T(8,128)S(1)}, f32[17,2,256,512]{3,2,1,0:T(8,128)}, s32[]{:T(128)}, s32[]{:T(128)}, /*index=5*/s32[]{:T(128)}) while((s32[]{:T(128)}, f32[2,256,512]{2,1,0:T(8,128)S(1)}, f32[17,2,256,512]{3,2,1,0:T(8,128)}, s32[]{:T(128)}, s32[]{:T(128)}, /*index=5*/s32[]{:T(128)}) %tuple.109), condition=%wide.region_15.17_spmd, body=%wide.region_14.16_spmd.sunk | while | flops 262149 | bytes 7340179 | solution.py:110
  688.7 23.4 %collective-permute-done.1 = f32[2,256,512]{2,1,0:T(8,128)S(1)} collective-permute-done((f32[2,256,512]{2,1,0:T(8,128)S(1)}, f32[2,256,512]{2,1,0:T(8,128)S(1)}, u32[]{:S(2)}, u32[]{:S(2)}) %collective-permute-start.1) | collective-permute-done | bytes 1048608 | tf_op jit(solution)/shard_map/while/body/eval_jaxpr/ppermute | solution.py:16
  713.5 5.8 collective-permute-start.1
  719.4 21.6 %collective-permute-done.1 = f32[2,256,512]{2,1,0:T(8,128)S(1)} collective-permute-done((f32[2,256,512]{2,1,0:T(8,128)S(1)}, f32[2,256,512]{2,1,0:T(8,128)S(1)}, u32[]{:S(2)}, u32[]{:S(2)}) %collective-permute-start.1) | collective-permute-done | bytes 1048608 | tf_op jit(solution)/shard_map/while/body/eval_jaxpr/ppermute | solution.py:16
  742.4 6.8 collective-permute-start.1
  749.1 20.6 %collective-permute-done.1 = f32[2,256,512]{2,1,0:T(8,128)S(1)} collective-permute-done((f32[2,256,512]{2,1,0:T(8,128)S(1)}, f32[2,256,512]{2,1,0:T(8,128)S(1)}, u32[]{:S(2)}, u32[]{:S(2)}) %collective-permute-start.1) | collective-permute-done | bytes 1048608 | tf_op jit(solution)/shard_map/while/body/eval_jaxpr/ppermute | solution.py:16
  771.2 6.8 collective-permute-start.1
  778.0 19.7 %collective-permute-done.1 = f32[2,256,512]{2,1,0:T(8,128)S(1)} collective-permute-done((f32[2,256,512]{2,1,0:T(8,128)S(1)}, f32[2,256,512]{2,1,0:T(8,128)S(1)}, u32[]{:S(2)}, u32[]{:S(2)}) %collective-permute-start.1) | collective-permute-done | bytes 1048608 | tf_op jit(solution)/shard_map/while/body/eval_jaxpr/ppermute | solution.py:16
  799.1 6.8 collective-permute-start.1
  805.9 18.8 %collective-permute-done.1 = f32[2,256,512]{2,1,0:T(8,128)S(1)} collective-permute-done((f32[2,256,512]{2,1,0:T(8,128)S(1)}, f32[2,256,512]{2,1,0:T(8,128)S(1)}, u32[]{:S(2)}, u32[]{:S(2)}) %collective-permute-start.1) | collective-permute-done | bytes 1048608 | tf_op jit(solution)/shard_map/while/body/eval_jaxpr/ppermute | solution.py:16
  826.1 6.8 collective-permute-start.1
  832.9 17.9 %collective-permute-done.1 = f32[2,256,512]{2,1,0:T(8,128)S(1)} collective-permute-done((f32[2,256,512]{2,1,0:T(8,128)S(1)}, f32[2,256,512]{2,1,0:T(8,128)S(1)}, u32[]{:S(2)}, u32[]{:S(2)}) %collective-permute-start.1) | collective-permute-done | bytes 1048608 | tf_op jit(solution)/shard_map/while/body/eval_jaxpr/ppermute | solution.py:16
  852.2 6.8 collective-permute-start.1
  859.0 16.9 %collective-permute-done.1 = f32[2,256,512]{2,1,0:T(8,128)S(1)} collective-permute-done((f32[2,256,512]{2,1,0:T(8,128)S(1)}, f32[2,256,512]{2,1,0:T(8,128)S(1)}, u32[]{:S(2)}, u32[]{:S(2)}) %collective-permute-start.1) | collective-permute-done | bytes 1048608 | tf_op jit(solution)/shard_map/while/body/eval_jaxpr/ppermute | solution.py:16
  877.4 6.8 collective-permute-start.1
  884.2 16.0 %collective-permute-done.1 = f32[2,256,512]{2,1,0:T(8,128)S(1)} collective-permute-done((f32[2,256,512]{2,1,0:T(8,128)S(1)}, f32[2,256,512]{2,1,0:T(8,128)S(1)}, u32[]{:S(2)}, u32[]{:S(2)}) %collective-permute-start.1) | collective-permute-done | bytes 1048608 | tf_op jit(solution)/shard_map/while/body/eval_jaxpr/ppermute | solution.py:16
  901.6 6.8 collective-permute-start.1
  908.4 15.1 %collective-permute-done.1 = f32[2,256,512]{2,1,0:T(8,128)S(1)} collective-permute-done((f32[2,256,512]{2,1,0:T(8,128)S(1)}, f32[2,256,512]{2,1,0:T(8,128)S(1)}, u32[]{:S(2)}, u32[]{:S(2)}) %collective-permute-start.1) | collective-permute-done | bytes 1048608 | tf_op jit(solution)/shard_map/while/body/eval_jaxpr/ppermute | solution.py:16
  924.9 6.8 collective-permute-start.1
  931.7 15.1 %collective-permute-done.1 = f32[2,256,512]{2,1,0:T(8,128)S(1)} collective-permute-done((f32[2,256,512]{2,1,0:T(8,128)S(1)}, f32[2,256,512]{2,1,0:T(8,128)S(1)}, u32[]{:S(2)}, u32[]{:S(2)}) %collective-permute-start.1) | collective-permute-done | bytes 1048608 | tf_op jit(solution)/shard_map/while/body/eval_jaxpr/ppermute | solution.py:16
  948.3 6.8 collective-permute-start.1
  955.0 15.1 %collective-permute-done.1 = f32[2,256,512]{2,1,0:T(8,128)S(1)} collective-permute-done((f32[2,256,512]{2,1,0:T(8,128)S(1)}, f32[2,256,512]{2,1,0:T(8,128)S(1)}, u32[]{:S(2)}, u32[]{:S(2)}) %collective-permute-start.1) | collective-permute-done | bytes 1048608 | tf_op jit(solution)/shard_map/while/body/eval_jaxpr/ppermute | solution.py:16
  971.6 6.8 collective-permute-start.1
  978.4 15.1 %collective-permute-done.1 = f32[2,256,512]{2,1,0:T(8,128)S(1)} collective-permute-done((f32[2,256,512]{2,1,0:T(8,128)S(1)}, f32[2,256,512]{2,1,0:T(8,128)S(1)}, u32[]{:S(2)}, u32[]{:S(2)}) %collective-permute-start.1) | collective-permute-done | bytes 1048608 | tf_op jit(solution)/shard_map/while/body/eval_jaxpr/ppermute | solution.py:16
  994.9 6.8 collective-permute-start.1
  1001.7 16.0 %collective-permute-done.1 = f32[2,256,512]{2,1,0:T(8,128)S(1)} collective-permute-done((f32[2,256,512]{2,1,0:T(8,128)S(1)}, f32[2,256,512]{2,1,0:T(8,128)S(1)}, u32[]{:S(2)}, u32[]{:S(2)}) %collective-permute-start.1) | collective-permute-done | bytes 1048608 | tf_op jit(solution)/shard_map/while/body/eval_jaxpr/ppermute | solution.py:16
  1019.1 6.8 collective-permute-start.1
  1025.9 17.1 %collective-permute-done.1 = f32[2,256,512]{2,1,0:T(8,128)S(1)} collective-permute-done((f32[2,256,512]{2,1,0:T(8,128)S(1)}, f32[2,256,512]{2,1,0:T(8,128)S(1)}, u32[]{:S(2)}, u32[]{:S(2)}) %collective-permute-start.1) | collective-permute-done | bytes 1048608 | tf_op jit(solution)/shard_map/while/body/eval_jaxpr/ppermute | solution.py:16
  1044.4 6.8 collective-permute-start.1
  1051.2 18.1 %collective-permute-done.1 = f32[2,256,512]{2,1,0:T(8,128)S(1)} collective-permute-done((f32[2,256,512]{2,1,0:T(8,128)S(1)}, f32[2,256,512]{2,1,0:T(8,128)S(1)}, u32[]{:S(2)}, u32[]{:S(2)}) %collective-permute-start.1) | collective-permute-done | bytes 1048608 | tf_op jit(solution)/shard_map/while/body/eval_jaxpr/ppermute | solution.py:16
  1070.7 6.8 collective-permute-start.1
  1077.5 12.3 %collective-permute-done.1 = f32[2,256,512]{2,1,0:T(8,128)S(1)} collective-permute-done((f32[2,256,512]{2,1,0:T(8,128)S(1)}, f32[2,256,512]{2,1,0:T(8,128)S(1)}, u32[]{:S(2)}, u32[]{:S(2)}) %collective-permute-start.1) | collective-permute-done | bytes 1048608 | tf_op jit(solution)/shard_map/while/body/eval_jaxpr/ppermute | solution.py:16
  (286 shorter events, 252.5 us)
Async XLA Ops:
  0.6 10.1 copy-start.19
  2.6 14.6 %collective-permute-start.2 = (bf16[2,256,512]{2,1,0:T(8,128)(2,1)}, bf16[2,256,512]{2,1,0:T(8,128)(2,1)}, u32[]{:S(2)}, u32[]{:S(2)}) collective-permute-start(bf16[2,256,512]{2,1,0:T(8,128)(2,1)} %pad_maximum_fusion.2), channel_id=1, source_target_pairs={{32,0},{36,4},{40,8},{44,12},{48,16},{52,20},{56,24},{60,28},{64,3... | collective-permute-start | bytes 1572872 | tf_op jit(solution)/shard_map/ppermute | solution.py:16
  22.7 18.5 %collective-permute-start = (bf16[2,256,512]{2,1,0:T(8,128)(2,1)}, bf16[2,256,512]{2,1,0:T(8,128)(2,1)S(1)}, u32[]{:S(2)}, u32[]{:S(2)}) collective-permute-start(bf16[2,256,512]{2,1,0:T(8,128)(2,1)} %get-tuple-element.288), channel_id=1, source_target_pairs={{124,0},{0,4},{4,8},{8,12},{12,16},{16,20},{20,24},{24,28},{28,32}... | collective-permute-start | bytes 1572872 | tf_op jit(solution)/shard_map/while/body/eval_jaxpr/ppermute | solution.py:16
  42.9 16.6 %collective-permute-start = (bf16[2,256,512]{2,1,0:T(8,128)(2,1)}, bf16[2,256,512]{2,1,0:T(8,128)(2,1)S(1)}, u32[]{:S(2)}, u32[]{:S(2)}) collective-permute-start(bf16[2,256,512]{2,1,0:T(8,128)(2,1)} %get-tuple-element.288), channel_id=1, source_target_pairs={{124,0},{0,4},{4,8},{8,12},{12,16},{16,20},{20,24},{24,28},{28,32}... | collective-permute-start | bytes 1572872 | tf_op jit(solution)/shard_map/while/body/eval_jaxpr/ppermute | solution.py:16
  61.2 15.7 %collective-permute-start = (bf16[2,256,512]{2,1,0:T(8,128)(2,1)}, bf16[2,256,512]{2,1,0:T(8,128)(2,1)S(1)}, u32[]{:S(2)}, u32[]{:S(2)}) collective-permute-start(bf16[2,256,512]{2,1,0:T(8,128)(2,1)} %get-tuple-element.288), channel_id=1, source_target_pairs={{124,0},{0,4},{4,8},{8,12},{12,16},{16,20},{20,24},{24,28},{28,32}... | collective-permute-start | bytes 1572872 | tf_op jit(solution)/shard_map/while/body/eval_jaxpr/ppermute | solution.py:16
  78.5 14.7 %collective-permute-start = (bf16[2,256,512]{2,1,0:T(8,128)(2,1)}, bf16[2,256,512]{2,1,0:T(8,128)(2,1)S(1)}, u32[]{:S(2)}, u32[]{:S(2)}) collective-permute-start(bf16[2,256,512]{2,1,0:T(8,128)(2,1)} %get-tuple-element.288), channel_id=1, source_target_pairs={{124,0},{0,4},{4,8},{8,12},{12,16},{16,20},{20,24},{24,28},{28,32}... | collective-permute-start | bytes 1572872 | tf_op jit(solution)/shard_map/while/body/eval_jaxpr/ppermute | solution.py:16
  94.8 13.8 %collective-permute-start = (bf16[2,256,512]{2,1,0:T(8,128)(2,1)}, bf16[2,256,512]{2,1,0:T(8,128)(2,1)S(1)}, u32[]{:S(2)}, u32[]{:S(2)}) collective-permute-start(bf16[2,256,512]{2,1,0:T(8,128)(2,1)} %get-tuple-element.288), channel_id=1, source_target_pairs={{124,0},{0,4},{4,8},{8,12},{12,16},{16,20},{20,24},{24,28},{28,32}... | collective-permute-start | bytes 1572872 | tf_op jit(solution)/shard_map/while/body/eval_jaxpr/ppermute | solution.py:16
  110.3 13.6 %collective-permute-start = (bf16[2,256,512]{2,1,0:T(8,128)(2,1)}, bf16[2,256,512]{2,1,0:T(8,128)(2,1)S(1)}, u32[]{:S(2)}, u32[]{:S(2)}) collective-permute-start(bf16[2,256,512]{2,1,0:T(8,128)(2,1)} %get-tuple-element.288), channel_id=1, source_target_pairs={{124,0},{0,4},{4,8},{8,12},{12,16},{16,20},{20,24},{24,28},{28,32}... | collective-permute-start | bytes 1572872 | tf_op jit(solution)/shard_map/while/body/eval_jaxpr/ppermute | solution.py:16
  125.6 13.6 %collective-permute-start = (bf16[2,256,512]{2,1,0:T(8,128)(2,1)}, bf16[2,256,512]{2,1,0:T(8,128)(2,1)S(1)}, u32[]{:S(2)}, u32[]{:S(2)}) collective-permute-start(bf16[2,256,512]{2,1,0:T(8,128)(2,1)} %get-tuple-element.288), channel_id=1, source_target_pairs={{124,0},{0,4},{4,8},{8,12},{12,16},{16,20},{20,24},{24,28},{28,32}... | collective-permute-start | bytes 1572872 | tf_op jit(solution)/shard_map/while/body/eval_jaxpr/ppermute | solution.py:16
  140.9 13.7 %collective-permute-start = (bf16[2,256,512]{2,1,0:T(8,128)(2,1)}, bf16[2,256,512]{2,1,0:T(8,128)(2,1)S(1)}, u32[]{:S(2)}, u32[]{:S(2)}) collective-permute-start(bf16[2,256,512]{2,1,0:T(8,128)(2,1)} %get-tuple-element.288), channel_id=1, source_target_pairs={{124,0},{0,4},{4,8},{8,12},{12,16},{16,20},{20,24},{24,28},{28,32}... | collective-permute-start | bytes 1572872 | tf_op jit(solution)/shard_map/while/body/eval_jaxpr/ppermute | solution.py:16
  156.2 14.8 %collective-permute-start = (bf16[2,256,512]{2,1,0:T(8,128)(2,1)}, bf16[2,256,512]{2,1,0:T(8,128)(2,1)S(1)}, u32[]{:S(2)}, u32[]{:S(2)}) collective-permute-start(bf16[2,256,512]{2,1,0:T(8,128)(2,1)} %get-tuple-element.288), channel_id=1, source_target_pairs={{124,0},{0,4},{4,8},{8,12},{12,16},{16,20},{20,24},{24,28},{28,32}... | collective-permute-start | bytes 1572872 | tf_op jit(solution)/shard_map/while/body/eval_jaxpr/ppermute | solution.py:16
  172.6 15.8 %collective-permute-start = (bf16[2,256,512]{2,1,0:T(8,128)(2,1)}, bf16[2,256,512]{2,1,0:T(8,128)(2,1)S(1)}, u32[]{:S(2)}, u32[]{:S(2)}) collective-permute-start(bf16[2,256,512]{2,1,0:T(8,128)(2,1)} %get-tuple-element.288), channel_id=1, source_target_pairs={{124,0},{0,4},{4,8},{8,12},{12,16},{16,20},{20,24},{24,28},{28,32}... | collective-permute-start | bytes 1572872 | tf_op jit(solution)/shard_map/while/body/eval_jaxpr/ppermute | solution.py:16
  190.1 16.9 %collective-permute-start = (bf16[2,256,512]{2,1,0:T(8,128)(2,1)}, bf16[2,256,512]{2,1,0:T(8,128)(2,1)S(1)}, u32[]{:S(2)}, u32[]{:S(2)}) collective-permute-start(bf16[2,256,512]{2,1,0:T(8,128)(2,1)} %get-tuple-element.288), channel_id=1, source_target_pairs={{124,0},{0,4},{4,8},{8,12},{12,16},{16,20},{20,24},{24,28},{28,32}... | collective-permute-start | bytes 1572872 | tf_op jit(solution)/shard_map/while/body/eval_jaxpr/ppermute | solution.py:16
  208.7 18.1 %collective-permute-start = (bf16[2,256,512]{2,1,0:T(8,128)(2,1)}, bf16[2,256,512]{2,1,0:T(8,128)(2,1)S(1)}, u32[]{:S(2)}, u32[]{:S(2)}) collective-permute-start(bf16[2,256,512]{2,1,0:T(8,128)(2,1)} %get-tuple-element.288), channel_id=1, source_target_pairs={{124,0},{0,4},{4,8},{8,12},{12,16},{16,20},{20,24},{24,28},{28,32}... | collective-permute-start | bytes 1572872 | tf_op jit(solution)/shard_map/while/body/eval_jaxpr/ppermute | solution.py:16
  228.4 19.2 %collective-permute-start = (bf16[2,256,512]{2,1,0:T(8,128)(2,1)}, bf16[2,256,512]{2,1,0:T(8,128)(2,1)S(1)}, u32[]{:S(2)}, u32[]{:S(2)}) collective-permute-start(bf16[2,256,512]{2,1,0:T(8,128)(2,1)} %get-tuple-element.288), channel_id=1, source_target_pairs={{124,0},{0,4},{4,8},{8,12},{12,16},{16,20},{20,24},{24,28},{28,32}... | collective-permute-start | bytes 1572872 | tf_op jit(solution)/shard_map/while/body/eval_jaxpr/ppermute | solution.py:16
  249.3 18.4 %collective-permute-start = (bf16[2,256,512]{2,1,0:T(8,128)(2,1)}, bf16[2,256,512]{2,1,0:T(8,128)(2,1)S(1)}, u32[]{:S(2)}, u32[]{:S(2)}) collective-permute-start(bf16[2,256,512]{2,1,0:T(8,128)(2,1)} %get-tuple-element.288), channel_id=1, source_target_pairs={{124,0},{0,4},{4,8},{8,12},{12,16},{16,20},{20,24},{24,28},{28,32}... | collective-permute-start | bytes 1572872 | tf_op jit(solution)/shard_map/while/body/eval_jaxpr/ppermute | solution.py:16
  269.3 17.5 %collective-permute-start = (bf16[2,256,512]{2,1,0:T(8,128)(2,1)}, bf16[2,256,512]{2,1,0:T(8,128)(2,1)S(1)}, u32[]{:S(2)}, u32[]{:S(2)}) collective-permute-start(bf16[2,256,512]{2,1,0:T(8,128)(2,1)} %get-tuple-element.288), channel_id=1, source_target_pairs={{124,0},{0,4},{4,8},{8,12},{12,16},{16,20},{20,24},{24,28},{28,32}... | collective-permute-start | bytes 1572872 | tf_op jit(solution)/shard_map/while/body/eval_jaxpr/ppermute | solution.py:16
  288.5 13.6 %collective-permute-start = (bf16[2,256,512]{2,1,0:T(8,128)(2,1)}, bf16[2,256,512]{2,1,0:T(8,128)(2,1)S(1)}, u32[]{:S(2)}, u32[]{:S(2)}) collective-permute-start(bf16[2,256,512]{2,1,0:T(8,128)(2,1)} %get-tuple-element.288), channel_id=1, source_target_pairs={{124,0},{0,4},{4,8},{8,12},{12,16},{16,20},{20,24},{24,28},{28,32}... | collective-permute-start | bytes 1572872 | tf_op jit(solution)/shard_map/while/body/eval_jaxpr/ppermute | solution.py:16
  357.0 4.9 copy-start.14
  366.6 9.2 slice-start.6
  366.6 9.2 slice-start.12
  366.6 9.2 slice-start.7
  366.6 9.2 slice-start.13
  390.8 4.9 copy-start.13
  400.5 9.2 slice-start.8
  400.5 9.2 slice-start.14
  400.5 9.2 slice-start.9
  400.5 9.2 slice-start.15
  424.9 4.9 copy-start.12
  434.6 9.2 slice-start.10
  434.6 9.2 slice-start.16
  434.6 9.2 slice-start.11
  434.6 9.2 slice-start.17
  438.3 4.1 copy-start.10
  497.0 4.5 copy-start.5
  497.0 4.5 copy-start.6
  497.0 5.6 copy-start.11
  506.5 8.4 copy-start.15
  511.3 6.7 slice-start.4
  511.3 6.7 slice-start.18
  511.3 7.0 slice-start.5
  511.3 7.8 slice-start.19
  609.4 8.0 copy-start.27
  628.2 5.9 slice-start
  686.7 25.4 %collective-permute-start.1 = (f32[2,256,512]{2,1,0:T(8,128)S(1)}, f32[2,256,512]{2,1,0:T(8,128)S(1)}, u32[]{:S(2)}, u32[]{:S(2)}) collective-permute-start(f32[2,256,512]{2,1,0:T(8,128)S(1)} %get-tuple-element.308), channel_id=1, source_target_pairs={{4,0},{8,4},{12,8},{16,12},{20,16},{24,20},{28,24},{32,28},{36,32}... | collective-permute-start | bytes 3145736 | tf_op jit(solution)/shard_map/while/body/eval_jaxpr/ppermute | solution.py:16
  713.5 27.4 %collective-permute-start.1 = (f32[2,256,512]{2,1,0:T(8,128)S(1)}, f32[2,256,512]{2,1,0:T(8,128)S(1)}, u32[]{:S(2)}, u32[]{:S(2)}) collective-permute-start(f32[2,256,512]{2,1,0:T(8,128)S(1)} %get-tuple-element.308), channel_id=1, source_target_pairs={{4,0},{8,4},{12,8},{16,12},{20,16},{24,20},{28,24},{32,28},{36,32}... | collective-permute-start | bytes 3145736 | tf_op jit(solution)/shard_map/while/body/eval_jaxpr/ppermute | solution.py:16
  742.4 27.4 %collective-permute-start.1 = (f32[2,256,512]{2,1,0:T(8,128)S(1)}, f32[2,256,512]{2,1,0:T(8,128)S(1)}, u32[]{:S(2)}, u32[]{:S(2)}) collective-permute-start(f32[2,256,512]{2,1,0:T(8,128)S(1)} %get-tuple-element.308), channel_id=1, source_target_pairs={{4,0},{8,4},{12,8},{16,12},{20,16},{24,20},{28,24},{32,28},{36,32}... | collective-permute-start | bytes 3145736 | tf_op jit(solution)/shard_map/while/body/eval_jaxpr/ppermute | solution.py:16
  771.2 26.5 %collective-permute-start.1 = (f32[2,256,512]{2,1,0:T(8,128)S(1)}, f32[2,256,512]{2,1,0:T(8,128)S(1)}, u32[]{:S(2)}, u32[]{:S(2)}) collective-permute-start(f32[2,256,512]{2,1,0:T(8,128)S(1)} %get-tuple-element.308), channel_id=1, source_target_pairs={{4,0},{8,4},{12,8},{16,12},{20,16},{24,20},{28,24},{32,28},{36,32}... | collective-permute-start | bytes 3145736 | tf_op jit(solution)/shard_map/while/body/eval_jaxpr/ppermute | solution.py:16
  799.1 25.6 %collective-permute-start.1 = (f32[2,256,512]{2,1,0:T(8,128)S(1)}, f32[2,256,512]{2,1,0:T(8,128)S(1)}, u32[]{:S(2)}, u32[]{:S(2)}) collective-permute-start(f32[2,256,512]{2,1,0:T(8,128)S(1)} %get-tuple-element.308), channel_id=1, source_target_pairs={{4,0},{8,4},{12,8},{16,12},{20,16},{24,20},{28,24},{32,28},{36,32}... | collective-permute-start | bytes 3145736 | tf_op jit(solution)/shard_map/while/body/eval_jaxpr/ppermute | solution.py:16
  826.1 24.6 %collective-permute-start.1 = (f32[2,256,512]{2,1,0:T(8,128)S(1)}, f32[2,256,512]{2,1,0:T(8,128)S(1)}, u32[]{:S(2)}, u32[]{:S(2)}) collective-permute-start(f32[2,256,512]{2,1,0:T(8,128)S(1)} %get-tuple-element.308), channel_id=1, source_target_pairs={{4,0},{8,4},{12,8},{16,12},{20,16},{24,20},{28,24},{32,28},{36,32}... | collective-permute-start | bytes 3145736 | tf_op jit(solution)/shard_map/while/body/eval_jaxpr/ppermute | solution.py:16
  852.2 23.7 %collective-permute-start.1 = (f32[2,256,512]{2,1,0:T(8,128)S(1)}, f32[2,256,512]{2,1,0:T(8,128)S(1)}, u32[]{:S(2)}, u32[]{:S(2)}) collective-permute-start(f32[2,256,512]{2,1,0:T(8,128)S(1)} %get-tuple-element.308), channel_id=1, source_target_pairs={{4,0},{8,4},{12,8},{16,12},{20,16},{24,20},{28,24},{32,28},{36,32}... | collective-permute-start | bytes 3145736 | tf_op jit(solution)/shard_map/while/body/eval_jaxpr/ppermute | solution.py:16
  877.4 22.8 %collective-permute-start.1 = (f32[2,256,512]{2,1,0:T(8,128)S(1)}, f32[2,256,512]{2,1,0:T(8,128)S(1)}, u32[]{:S(2)}, u32[]{:S(2)}) collective-permute-start(f32[2,256,512]{2,1,0:T(8,128)S(1)} %get-tuple-element.308), channel_id=1, source_target_pairs={{4,0},{8,4},{12,8},{16,12},{20,16},{24,20},{28,24},{32,28},{36,32}... | collective-permute-start | bytes 3145736 | tf_op jit(solution)/shard_map/while/body/eval_jaxpr/ppermute | solution.py:16
  901.6 21.9 %collective-permute-start.1 = (f32[2,256,512]{2,1,0:T(8,128)S(1)}, f32[2,256,512]{2,1,0:T(8,128)S(1)}, u32[]{:S(2)}, u32[]{:S(2)}) collective-permute-start(f32[2,256,512]{2,1,0:T(8,128)S(1)} %get-tuple-element.308), channel_id=1, source_target_pairs={{4,0},{8,4},{12,8},{16,12},{20,16},{24,20},{28,24},{32,28},{36,32}... | collective-permute-start | bytes 3145736 | tf_op jit(solution)/shard_map/while/body/eval_jaxpr/ppermute | solution.py:16
  924.9 21.9 %collective-permute-start.1 = (f32[2,256,512]{2,1,0:T(8,128)S(1)}, f32[2,256,512]{2,1,0:T(8,128)S(1)}, u32[]{:S(2)}, u32[]{:S(2)}) collective-permute-start(f32[2,256,512]{2,1,0:T(8,128)S(1)} %get-tuple-element.308), channel_id=1, source_target_pairs={{4,0},{8,4},{12,8},{16,12},{20,16},{24,20},{28,24},{32,28},{36,32}... | collective-permute-start | bytes 3145736 | tf_op jit(solution)/shard_map/while/body/eval_jaxpr/ppermute | solution.py:16
  948.3 21.9 %collective-permute-start.1 = (f32[2,256,512]{2,1,0:T(8,128)S(1)}, f32[2,256,512]{2,1,0:T(8,128)S(1)}, u32[]{:S(2)}, u32[]{:S(2)}) collective-permute-start(f32[2,256,512]{2,1,0:T(8,128)S(1)} %get-tuple-element.308), channel_id=1, source_target_pairs={{4,0},{8,4},{12,8},{16,12},{20,16},{24,20},{28,24},{32,28},{36,32}... | collective-permute-start | bytes 3145736 | tf_op jit(solution)/shard_map/while/body/eval_jaxpr/ppermute | solution.py:16
  971.6 21.9 %collective-permute-start.1 = (f32[2,256,512]{2,1,0:T(8,128)S(1)}, f32[2,256,512]{2,1,0:T(8,128)S(1)}, u32[]{:S(2)}, u32[]{:S(2)}) collective-permute-start(f32[2,256,512]{2,1,0:T(8,128)S(1)} %get-tuple-element.308), channel_id=1, source_target_pairs={{4,0},{8,4},{12,8},{16,12},{20,16},{24,20},{28,24},{32,28},{36,32}... | collective-permute-start | bytes 3145736 | tf_op jit(solution)/shard_map/while/body/eval_jaxpr/ppermute | solution.py:16
  994.9 22.7 %collective-permute-start.1 = (f32[2,256,512]{2,1,0:T(8,128)S(1)}, f32[2,256,512]{2,1,0:T(8,128)S(1)}, u32[]{:S(2)}, u32[]{:S(2)}) collective-permute-start(f32[2,256,512]{2,1,0:T(8,128)S(1)} %get-tuple-element.308), channel_id=1, source_target_pairs={{4,0},{8,4},{12,8},{16,12},{20,16},{24,20},{28,24},{32,28},{36,32}... | collective-permute-start | bytes 3145736 | tf_op jit(solution)/shard_map/while/body/eval_jaxpr/ppermute | solution.py:16
  1019.1 23.8 %collective-permute-start.1 = (f32[2,256,512]{2,1,0:T(8,128)S(1)}, f32[2,256,512]{2,1,0:T(8,128)S(1)}, u32[]{:S(2)}, u32[]{:S(2)}) collective-permute-start(f32[2,256,512]{2,1,0:T(8,128)S(1)} %get-tuple-element.308), channel_id=1, source_target_pairs={{4,0},{8,4},{12,8},{16,12},{20,16},{24,20},{28,24},{32,28},{36,32}... | collective-permute-start | bytes 3145736 | tf_op jit(solution)/shard_map/while/body/eval_jaxpr/ppermute | solution.py:16
  1044.4 24.9 %collective-permute-start.1 = (f32[2,256,512]{2,1,0:T(8,128)S(1)}, f32[2,256,512]{2,1,0:T(8,128)S(1)}, u32[]{:S(2)}, u32[]{:S(2)}) collective-permute-start(f32[2,256,512]{2,1,0:T(8,128)S(1)} %get-tuple-element.308), channel_id=1, source_target_pairs={{4,0},{8,4},{12,8},{16,12},{20,16},{24,20},{28,24},{32,28},{36,32}... | collective-permute-start | bytes 3145736 | tf_op jit(solution)/shard_map/while/body/eval_jaxpr/ppermute | solution.py:16
  1070.7 19.1 %collective-permute-start.1 = (f32[2,256,512]{2,1,0:T(8,128)S(1)}, f32[2,256,512]{2,1,0:T(8,128)S(1)}, u32[]{:S(2)}, u32[]{:S(2)}) collective-permute-start(f32[2,256,512]{2,1,0:T(8,128)S(1)} %get-tuple-element.308), channel_id=1, source_target_pairs={{4,0},{8,4},{12,8},{16,12},{20,16},{24,20},{28,24},{32,28},{36,32}... | collective-permute-start | bytes 3145736 | tf_op jit(solution)/shard_map/while/body/eval_jaxpr/ppermute | solution.py:16
  1091.3 4.9 copy-start.20
  1091.3 4.9 copy-start.21
  1091.3 4.9 copy-start.22
  1092.2 10.9 collective-permute-start.3
  (18 other events, 51.9 us)
